TPU v7x, 256 devices: a whole 4x4x8 slice. The times are simulated.
256 devices in a mesh: ctx: 16 (over z_lo, y), fsdp: 16 (over z_hi, x, core).
Axes of the slice: x: 4, y: 4, z: 8 (z_hi: 2, z_lo: 4; z = z_hi * 4 + z_lo), core: 2. Of those that a mesh axis runs over, the one named last changes fastest.
Arguments:
- inputs: bfloat16 [4096, 7168], P('ctx'), may hold values from -12 to 12
- w_qkv: bfloat16 [7168, 3, 4096], P('ctx', None, 'fsdp'), may hold values from -1 to 1, as said below
- selected: int32 [8, 4], replicated, may hold values from -1 to 7, as said below
- d_attn: bfloat16 [4096, 4096], P('ctx', 'fsdp'), may hold values from -6 to 6
Outputs:
- d_input: bfloat16 [4096, 7168], P('ctx', 'fsdp')
Inputs may be any that keep to these rules, and one draw needn't show every extreme that they name: `selected`: row b lists min(b + 1, 4) different blocks of 0 to b, b among them, in the first slots; the other slots hold -1. `w_qkv`: projection weights scaled by the fan-in.
All inputs are finite; a program needn't handle non-finite values.
Results may differ from a plain program's by a relative error of at most 0.023.
Values may be sent and summed in bfloat16 or wider, within the bound.
A program may use at most 128 MiB of HBM per device.

v0:
```python
import jax
import jax.numpy as jnp
from jax import lax
from jax.sharding import PartitionSpec as P

HD = 128
BLOCK = 512


def stat_rows(stat, row_count, heads):
    return stat[..., 0].transpose(0, 2, 1).reshape(row_count, heads)


def attend_chosen(query, keys_all, values_all, grad_out, selected, first_row):
    row_count, col_count = query.shape
    seq_len = keys_all.shape[0]
    nblocks = seq_len // BLOCK
    heads = col_count // HD
    top_count = selected.shape[1]
    group = min(BLOCK, row_count)
    groups = row_count // group
    scaling = HD ** (-0.5)
    block_ids = jnp.arange(nblocks, dtype=jnp.int32)
    q_block = (first_row + jnp.arange(groups, dtype=jnp.int32) * group) // BLOCK
    picked = q_block[:, None] == block_ids[None, :]
    chosen_ids = jnp.sum(jnp.where(picked[:, :, None], selected[None], 0), axis=1)
    index = jnp.maximum(chosen_ids, 0)
    key_pos = index[:, :, None] * BLOCK + jnp.arange(BLOCK, dtype=jnp.int32)[None, None, :]
    key_pos = key_pos.reshape(groups, top_count * BLOCK)
    slot_valid = jnp.repeat(chosen_ids >= 0, BLOCK, axis=1)
    position_q = (first_row + jnp.arange(row_count, dtype=jnp.int32)).reshape(groups, group)
    allowed = slot_valid[:, None, :] & (position_q[:, :, None] >= key_pos[:, None, :])
    key_heads = keys_all.reshape(nblocks, BLOCK, col_count)[index].reshape(
        groups, top_count * BLOCK, heads, HD
    )
    value_heads = values_all.reshape(nblocks, BLOCK, col_count)[index].reshape(
        groups, top_count * BLOCK, heads, HD
    )
    query_heads = query.reshape(groups, group, heads, HD)
    grad_heads = grad_out.reshape(groups, group, heads, HD)
    scores = (
        jnp.einsum("bqhd,bkhd->bhqk", query_heads, key_heads, preferred_element_type=jnp.float32)
        * scaling
    )
    masked = jnp.where(allowed[:, None], scores, -jnp.inf)
    highest = jnp.max(masked, axis=-1, keepdims=True)
    expo = jnp.exp(masked - highest)
    totals = jnp.sum(expo, axis=-1, keepdims=True)
    probs = expo / totals
    probs_low = probs.astype(jnp.bfloat16)
    attended = jnp.einsum(
        "bhqk,bkhd->bqhd", probs_low, value_heads, preferred_element_type=jnp.float32
    ).astype(jnp.bfloat16)
    delta_rows = jnp.sum(grad_heads.astype(jnp.float32) * attended.astype(jnp.float32), axis=3)
    delta = delta_rows.transpose(0, 2, 1)[..., None]
    dprobs = jnp.einsum(
        "bqhd,bkhd->bhqk", grad_heads, value_heads, preferred_element_type=jnp.float32
    )
    dscores = (probs * (dprobs - delta)).astype(jnp.bfloat16)
    dquery = (
        jnp.einsum("bhqk,bkhd->bqhd", dscores, key_heads, preferred_element_type=jnp.float32)
        * scaling
    )
    dquery = dquery.astype(jnp.bfloat16).reshape(row_count, col_count)
    highest_rows = stat_rows(highest, row_count, heads)
    total_rows = stat_rows(totals, row_count, heads)
    delta_flat = delta_rows.reshape(row_count, heads)
    key_slots = (
        jnp.einsum("bhqk,bqhd->bkhd", dscores, query_heads, preferred_element_type=jnp.float32)
        * scaling
    )
    value_slots = jnp.einsum(
        "bhqk,bqhd->bkhd", probs_low, grad_heads, preferred_element_type=jnp.float32
    )
    onehot = (chosen_ids[:, :, None] == block_ids[None, None, :]).astype(jnp.float32)
    key_term = jnp.einsum(
        "gtn,gtkc->nkc",
        onehot,
        key_slots.reshape(groups, top_count, BLOCK, col_count),
        precision=lax.Precision.HIGHEST,
    ).reshape(seq_len, col_count)
    value_term = jnp.einsum(
        "gtn,gtkc->nkc",
        onehot,
        value_slots.reshape(groups, top_count, BLOCK, col_count),
        precision=lax.Precision.HIGHEST,
    ).reshape(seq_len, col_count)
    return (dquery, key_term, value_term, highest_rows, total_rows, delta_flat)


def shards(inputs, w_qkv, selected, d_attn):
    row_count, width = inputs.shape
    col_count = w_qkv.shape[2]
    first_row = lax.axis_index("ctx") * row_count
    whole_w = lax.all_gather(w_qkv, "ctx", axis=0, tiled=True).reshape(width, 3 * col_count)
    projected = jnp.dot(inputs, whole_w, preferred_element_type=jnp.float32)
    projected = projected.astype(jnp.bfloat16).reshape(row_count, 3, col_count)
    query = projected[:, 0]
    keys_local = projected[:, 1]
    values_local = projected[:, 2]
    keys_all, values_all = (
        lax.all_gather(keys_local, "ctx", axis=0, tiled=True),
        lax.all_gather(values_local, "ctx", axis=0, tiled=True),
    )
    dquery, key_term, value_term, _, _, _ = attend_chosen(
        query, keys_all, values_all, d_attn, selected, first_row
    )
    key_total, value_total = (
        lax.psum_scatter(
            key_term.astype(jnp.bfloat16), "ctx", scatter_dimension=0, tiled=True
        ).astype(jnp.float32),
        lax.psum_scatter(
            value_term.astype(jnp.bfloat16), "ctx", scatter_dimension=0, tiled=True
        ).astype(jnp.float32),
    )
    key_sum = key_total.astype(jnp.bfloat16)
    value_sum = value_total.astype(jnp.bfloat16)
    flat_grads = jnp.stack([dquery, key_sum, value_sum], axis=1).reshape(row_count, 3 * col_count)
    contract = (((1,), (1,)), ((), ()))
    partial_grad = lax.dot_general(
        flat_grads, whole_w, contract, preferred_element_type=jnp.float32
    )
    total = lax.psum_scatter(
        partial_grad.astype(jnp.bfloat16), "fsdp", scatter_dimension=1, tiled=True
    )
    return total


def solution(mesh):
    placed = (P("ctx", None), P("ctx", None, "fsdp"), P(), P("ctx", "fsdp"))
    return jax.shard_map(
        shards, mesh=mesh, in_specs=placed, out_specs=P("ctx", "fsdp"), check_vma=False
    )
```

profile of v0, /device:TPU:8, one launch (start us, length us, event | category | flops | bytes accessed | tf_op | source)
XLA Modules:
  0.0 630.6 jit_solution(6221910780856533034)
XLA Ops:
  6.5 0.7 all-gather.6.cloned.1.call-update
  7.3 129.8 %all-gather.6.cloned.1.call-done = bf16[7168,3,256]{2,0,1:T(8,128)(2,1)} async-done(((bf16[448,3,256]{2,0,1:T(8,128)(2,1)}), bf16[7168,3,256]{2,0,1:T(8,128)(2,1)}) %all-gather.6.cloned.1.call-update) | async-done | bytes 11010064 | tf_op jit(solution)/shard_map/all_gather | solution.py:95
  137.1 14.8 %copy.15 = bf16[7168,3,256]{0,2,1:T(8,128)(2,1)} copy(bf16[7168,3,256]{2,0,1:T(8,128)(2,1)} %all-gather.6.cloned.1.call-done) | data formatting | bytes 22020096 | tf_op jit(solution)/shard_map/all_gather | solution.py:95
  151.9 8.3 %convolution_convert_fusion.1 = bf16[256,768]{1,0:T(8,128)(2,1)S(1)} fusion(bf16[256,7168]{1,0:T(8,128)(2,1)} %param.4, bf16[7168,768]{0,1:T(8,128)(2,1)} %bitcast.100), kind=kOutput, calls=%fused_computation.23 | convolution fusion | flops 2818768896 | bytes 15073280 | tf_op jit(solution)/shard_map/dot_general | solution.py:96
  160.2 0.2 copy.16
  160.4 0.7 fusion.39
  161.1 0.0 all-gather.10.cloned.1.call-start
  161.2 0.7 all-gather.10.cloned.1.call-update
  161.9 0.2 reduce-scatter.4.cloned.1.call-start
  162.2 0.1 select_reduce_fusion
  162.3 0.1 broadcast_bitcast_fusion
  162.4 0.1 copy.23
  162.5 0.1 add.48
  162.6 1.2 compare_and_fusion
  163.8 71.9 %all-gather.8.cloned.1.call-done = bf16[4096,1,256]{0,2,1:T(8,128)(2,1)} async-done(((bf16[256,1,256]{0,2,1:T(8,128)(2,1)}), bf16[4096,1,256]{0,2,1:T(8,128)(2,1)}) %all-gather.8.cloned.1.call-update) | async-done | bytes 2097168 | tf_op jit(solution)/shard_map/all_gather | solution.py:102
  235.7 3.3 copy.17
  239.0 0.6 gather_fusion
  239.6 0.3 reshape.318
  239.9 0.8 copy.26
  240.7 70.2 %all-gather.10.cloned.1.call-done = bf16[4096,1,256]{0,2,1:T(8,128)(2,1)} async-done(((bf16[256,1,256]{0,2,1:T(8,128)(2,1)}), bf16[4096,1,256]{0,2,1:T(8,128)(2,1)}) %all-gather.10.cloned.1.call-update) | async-done | bytes 2097168 | tf_op jit(solution)/shard_map/all_gather | solution.py:103
  310.9 3.3 copy.20
  314.2 1.6 gather_fusion.1
  315.8 1.4 reshape.321
  317.2 2.1 copy.24
  319.3 3.7 fusion.40
  322.9 2.9 fusion.13
  325.9 0.9 fusion.19
  326.7 0.7 fusion.2
  327.5 1.4 copy-done
  328.9 1.8 fusion.4
  330.7 3.6 reshape.323
  334.3 4.1 copy.27
  338.4 4.1 convolution_convert_fusion
  342.5 1.7 copy.28
  344.3 0.3 reduce-scatter.6.cloned.1.call-start
  344.5 0.9 convolution_bitcast_fusion.1
  345.5 8.6 %copy.31 = f32[1,2048,2,128]{3,2,1,0:T(2,128)} copy(f32[1,2048,2,128]{3,1,2,0:T(8,128)S(1)} %convolution_bitcast_fusion.1) | data formatting | bytes 4194304 | tf_op jit(solution)/shard_map/bhqk,bqhd->bkhd/transpose | solution.py:72
  354.0 2.9 reshape.324
  357.0 3.4 fusion.10
  360.3 1.7 copy.33
  362.1 0.0 reduce-scatter.8.cloned.1.call-start
  362.1 1.5 copy-done.1
  363.7 0.8 fusion.14
  364.5 0.1 copy.34
  364.6 63.0 %reduce-scatter.4.cloned.1.call-done = bf16[256,256]{1,0:T(8,128)(2,1)} async-done(((bf16[4096,256]{1,0:T(8,128)(2,1)}), bf16[256,256]{1,0:T(8,128)(2,1)}) %reduce-scatter.4.cloned.1.call-update) | async-done | bytes 131088 | tf_op jit(solution)/shard_map/reduce_scatter | solution.py:109
  427.6 86.7 %reduce-scatter.6.cloned.1.call-done = bf16[256,256]{1,0:T(8,128)(2,1)} async-done(((bf16[4096,256]{1,0:T(8,128)(2,1)}), bf16[256,256]{1,0:T(8,128)(2,1)}) %reduce-scatter.6.cloned.1.call-update) | async-done | bytes 131088 | tf_op jit(solution)/shard_map/reduce_scatter | solution.py:112
  514.2 9.3 %fusion.1 = bf16[256,7168]{0,1:T(8,128)(2,1)} fusion(bf16[7168,3,256]{2,0,1:T(8,128)(2,1)} %all-gather.6.cloned.1.call-done, bf16[256,1,256]{2,0,1:T(8,128)(2,1)} %bitcast.115, bf16[256,1,256]{2,0,1:T(8,128)(2,1)} %bitcast.114, bf16[256,1,256]{2,0,1:T(8,128)(2,1)S(1)} %copy.34), kind=kOutput, calls=%fused_computation.4 | convolution fusion | flops 2820800512 | bytes 15073280 | tf_op jit(solution)/shard_map/dot_general | solution.py:120
  523.5 100.3 %reduce-scatter.8.cloned.1.call-done = bf16[256,448]{0,1:T(8,128)(2,1)} async-done(((bf16[256,7168]{0,1:T(8,128)(2,1)}), bf16[256,448]{0,1:T(8,128)(2,1)}) %reduce-scatter.8.cloned.1.call-update) | async-done | bytes 229392 | tf_op jit(solution)/shard_map/reduce_scatter | solution.py:123
  (31 shorter events, 0.2 us)
Async XLA Ops:
  6.5 130.5 %all-gather.6.cloned.1.call-start = ((), (), s32[]{:S(2)}) async-start(), calls=%async_computation.3 | async-start | bytes 11698176 | tf_op jit(solution)/shard_map/all_gather | solution.py:95
  7.3 228.4 %all-gather.8.cloned.1.call-start = ((), (), s32[]{:S(2)}) async-start(), calls=%async_computation.7 | async-start | bytes 2228224 | tf_op jit(solution)/shard_map/all_gather | solution.py:102
  151.9 10.3 %copy-start.8 = (s32[8,4]{0,1:T(4,128)S(1)}, s32[8,4]{0,1:T(4,128)}, u32[]{:S(2)}) copy-start(s32[8,4]{0,1:T(4,128)} %param.6) | copy-start | bytes 388
  151.9 10.5 %copy-start.4 = (bf16[256,256]{1,0:T(8,128)(2,1)S(1)}, bf16[256,256]{1,0:T(8,128)(2,1)}, u32[]{:S(2)}) copy-start(bf16[256,256]{1,0:T(8,128)(2,1)} %param.7) | copy-start | bytes 393220
  161.1 149.8 %all-gather.10.cloned.1.call-start = ((), (), s32[]{:S(2)}) async-start(), calls=%async_computation.8 | async-start | bytes 2228224 | tf_op jit(solution)/shard_map/all_gather | solution.py:103
  161.9 265.7 %reduce-scatter.4.cloned.1.call-start = ((), (), s32[]{:S(2)}) async-start(), calls=%async_computation.4 | async-start | bytes 2228224 | tf_op jit(solution)/shard_map/reduce_scatter | solution.py:109
  315.8 3.5 copy-start.5
  315.8 3.5 copy-start.6
  322.9 3.0 copy-start.2
  322.9 3.8 copy-start.3
  326.7 2.1 copy-start.7
  327.5 1.4 copy-start
  344.3 170.0 %reduce-scatter.6.cloned.1.call-start = ((), (), s32[]{:S(2)}) async-start(), calls=%async_computation.5 | async-start | bytes 2228224 | tf_op jit(solution)/shard_map/reduce_scatter | solution.py:112
  362.1 1.6 copy-start.1
  362.1 261.7 %reduce-scatter.8.cloned.1.call-start = ((), (), s32[]{:S(2)}) async-start(), calls=%async_computation.6 | async-start | bytes 3899392 | tf_op jit(solution)/shard_map/reduce_scatter | solution.py:123
Sparse Core Ops, SparseCore 0:
  9.1 127.8 all-gather.5
  161.2 74.3 all-gather.7
  237.4 73.4 all-gather.9
  344.4 83.1 reduce-scatter.3
  430.0 84.2 reduce-scatter.5
  523.6 100.1 reduce-scatter.7
where the time goes:
time: 631 us
  waiting for transfers between devices  523 us (83%)
  local copies, waits for them, and re-layouts  55 us (9%)
  matrix products  33.8 us (5%)
  between operations  13.7 us (2%)
    all_gather x1, waiting for transfers between devices, shards(): lax.all_gather(w_qkv, 'ctx', axis=0, tiled=True)  130 us
    reduce_scatter x1, waiting for transfers between devices, shards(): lax.psum_scatter(partial_grad.astype(jnp.bfloat16), 'fsdp', scatter_dimen...  100 us
    reduce_scatter x1, waiting for transfers between devices, shards(): lax.psum_scatter(value_term.astype(jnp.bfloat16), 'ctx', scatter_dimensio...  86.7 us
    all_gather x1, waiting for transfers between devices, shards(): lax.all_gather(keys_local, 'ctx', axis=0, tiled=True)  71.9 us
    all_gather x1, waiting for transfers between devices, shards(): lax.all_gather(values_local, 'ctx', axis=0, tiled=True)  70.2 us
    reduce_scatter x1, waiting for transfers between devices, shards(): lax.psum_scatter(key_term.astype(jnp.bfloat16), 'ctx', scatter_dimension=...  63 us
    another operation x7, local copies, waits for them, and re-layouts  15.3 us
    all_gather x1, local copies, waits for them, and re-layouts, shards(): lax.all_gather(w_qkv, 'ctx', axis=0, tiled=True)  14.8 us
  transfers between devices with their start and end apart: 6, of which 6 were waited for; matrix products, arithmetic and copies ran while one was open for 4% of the time, Pallas kernels for 0%

commit v1 on v0

--- a/solution.py
+++ b/solution.py
@@ -5,6 +5,13 @@
 
 HD = 128
 BLOCK = 512
+
+
+def swapped_in(x, axis, dim):
+    size = lax.axis_size(axis)
+    tiles = jnp.stack([x for _ in range(size)])
+    tiles = lax.all_to_all(tiles, axis, split_axis=0, concat_axis=0)
+    return jnp.concatenate(tiles, axis=dim)
 
 
 def stat_rows(stat, row_count, heads):
@@ -92,7 +99,7 @@
     row_count, width = inputs.shape
     col_count = w_qkv.shape[2]
     first_row = lax.axis_index("ctx") * row_count
-    whole_w = lax.all_gather(w_qkv, "ctx", axis=0, tiled=True).reshape(width, 3 * col_count)
+    whole_w = swapped_in(w_qkv, "ctx", 0).reshape(width, 3 * col_count)
     projected = jnp.dot(inputs, whole_w, preferred_element_type=jnp.float32)
     projected = projected.astype(jnp.bfloat16).reshape(row_count, 3, col_count)
     query = projected[:, 0]

time: 631 us -> 779 us (1.23)
  blocking collectives: 0 us -> 248 us
  waiting for transfers between devices: 523 us -> 392 us
  local copies, waits for them, and re-layouts: 55 us -> 84 us
    all_to_all x0 -> x1, blocking collectives: none -> 248 us  [swapped_in(): tiles = lax.all_to_all(tiles, axis, split_axis=0, concat_axis=0)]
    all_gather x1 -> x0, waiting for transfers between devices: 130 us -> none  [shards(): lax.all_gather(w_qkv, 'ctx', axis=0, tiled=True)]
    another operation x7 -> x9, local copies, waits for them, and re-layouts: 15.3 us -> 42.7 us  [the longest x1 20.9 us: shards(): whole_w = swapped_in(w_qkv, 'ctx', 0).reshape(width, 3 * col_count)]
    all_to_all x0 -> x1, local copies, waits for them, and re-layouts: none -> 16.4 us  [swapped_in(): tiles = lax.all_to_all(tiles, axis, split_axis=0, concat_axis=0)]
    all_gather x1 -> x0, local copies, waits for them, and re-layouts: 14.8 us -> none  [shards(): lax.all_gather(w_qkv, 'ctx', axis=0, tiled=True)]
  transfers between devices with their start and end apart: 6 -> 5, of which waited for: 6 -> 5; matrix products, arithmetic and copies ran while one was open for 4% -> 3% of each run, Pallas kernels for 0% -> 0%
where the time goes in v1:
time: 779 us; the launch traced here: 778 us
  waiting for transfers between devices  392 us (50%)
  blocking collectives  248 us (32%)
  local copies, waits for them, and re-layouts  84 us (11%)
  matrix products  34.8 us (4%)
  between operations  13.4 us (2%)
    all_to_all x1, blocking collectives, swapped_in(): tiles = lax.all_to_all(tiles, axis, split_axis=0, concat_axis=0)  248 us
    reduce_scatter x1, waiting for transfers between devices, shards(): lax.psum_scatter(partial_grad.astype(jnp.bfloat16), 'fsdp', scatter_dimen...  100 us
    reduce_scatter x1, waiting for transfers between devices, shards(): lax.psum_scatter(value_term.astype(jnp.bfloat16), 'ctx', scatter_dimensio...  86.3 us
    all_gather x1, waiting for transfers between devices, shards(): lax.all_gather(keys_local, 'ctx', axis=0, tiled=True)  71.4 us
    all_gather x1, waiting for transfers between devices, shards(): lax.all_gather(values_local, 'ctx', axis=0, tiled=True)  70.2 us
    reduce_scatter x1, waiting for transfers between devices, shards(): lax.psum_scatter(key_term.astype(jnp.bfloat16), 'ctx', scatter_dimension=...  63 us
    another operation x1, local copies, waits for them, and re-layouts, shards(): whole_w = swapped_in(w_qkv, 'ctx', 0).reshape(width, 3 * col_count)  20.9 us
    all_to_all x1, local copies, waits for them, and re-layouts, swapped_in(): tiles = lax.all_to_all(tiles, axis, split_axis=0, concat_axis=0)  16.4 us
  transfers between devices with their start and end apart: 5, of which 5 were waited for; matrix products, arithmetic and copies ran while one was open for 3% of the time, Pallas kernels for 0%

profile of v1, /device:TPU:8, one launch (start us, length us, event | category | flops | bytes accessed | tf_op | source)
XLA Modules:
  0.0 777.7 jit_solution(1286070850764660699)
XLA Ops:
  6.5 6.6 stack.8
  13.1 247.6 %all_to_all.5 = bf16[16,448,3,256]{3,1,2,0:T(8,128)(2,1)} all-to-all(bf16[16,448,3,256]{3,1,2,0:T(8,128)(2,1)} %stack.8), channel_id=1, replica_groups=mesh['ctx'=16,'fsdp'=16] {'ctx'}, dimensions={0} | all-to-all | bytes 22020096 | tf_op jit(solution)/shard_map/all_to_all | solution.py:13
  260.7 16.4 %copy.56 = bf16[16,448,3,256]{1,0,3,2:T(8,128)(2,1)} copy(bf16[16,448,3,256]{3,1,2,0:T(8,128)(2,1)} %all_to_all.5) | data formatting | bytes 22020096 | tf_op jit(solution)/shard_map/all_to_all | solution.py:13
  277.1 20.9 %reshape_reshape.3 = bf16[7168,768]{0,1:T(8,128)(2,1)} reshape(bf16[16,448,3,256]{1,0,3,2:T(8,128)(2,1)} %copy.56) | data formatting | bytes 22020096 | tf_op jit(solution)/shard_map/reshape;reshape | solution.py:102
  298.0 8.3 %convolution_convert_fusion.2 = bf16[256,768]{1,0:T(8,128)(2,1)S(1)} fusion(bf16[256,7168]{1,0:T(8,128)(2,1)} %param.4, bf16[7168,768]{0,1:T(8,128)(2,1)} %reshape_reshape.3), kind=kOutput, calls=%fused_computation.22 | convolution fusion | flops 2818768896 | bytes 15073280 | tf_op jit(solution)/shard_map/dot_general | solution.py:103
  306.3 0.2 copy.57
  306.5 0.7 fusion.32
  307.3 0.7 all-gather.7.cloned.1.call-update
  308.0 0.2 reduce-scatter.4.cloned.1.call-start
  308.3 0.1 select_reduce_fusion
  308.5 0.1 copy.64
  308.7 1.2 compare_and_fusion
  309.9 71.4 %all-gather.5.cloned.1.call-done = bf16[4096,1,256]{0,2,1:T(8,128)(2,1)} async-done(((bf16[256,1,256]{0,2,1:T(8,128)(2,1)}), bf16[4096,1,256]{0,2,1:T(8,128)(2,1)}) %all-gather.5.cloned.1.call-update) | async-done | bytes 2097168 | tf_op jit(solution)/shard_map/all_gather | solution.py:109
  381.4 3.3 copy.58
  384.6 0.6 gather_fusion
  385.3 0.3 reshape.318
  385.6 0.8 copy.67
  386.4 70.2 %all-gather.7.cloned.1.call-done = bf16[4096,1,256]{0,2,1:T(8,128)(2,1)} async-done(((bf16[256,1,256]{0,2,1:T(8,128)(2,1)}), bf16[4096,1,256]{0,2,1:T(8,128)(2,1)}) %all-gather.7.cloned.1.call-update) | async-done | bytes 2097168 | tf_op jit(solution)/shard_map/all_gather | solution.py:110
  456.6 3.3 copy.61
  459.9 1.6 gather_fusion.1
  461.5 1.4 reshape.321
  462.9 2.1 copy.65
  464.9 3.5 fusion.33
  468.5 2.9 fusion.12
  471.4 0.8 fusion.18
  472.3 0.7 fusion.1
  473.0 1.3 copy-done
  474.4 1.8 fusion.3
  476.2 3.6 reshape.323
  479.8 4.1 copy.68
  483.9 4.1 convolution_convert_fusion.1
  488.0 1.7 copy.69
  489.8 0.3 reduce-scatter.6.cloned.1.call-start
  490.0 0.9 convolution_bitcast_fusion
  491.0 8.6 %copy.72 = f32[1,2048,2,128]{3,2,1,0:T(2,128)} copy(f32[1,2048,2,128]{3,1,2,0:T(8,128)S(1)} %convolution_bitcast_fusion) | data formatting | bytes 4194304 | tf_op jit(solution)/shard_map/bhqk,bqhd->bkhd/transpose | solution.py:79
  499.6 2.9 reshape.324
  502.5 3.4 fusion.9
  505.9 1.7 copy.74
  507.6 0.3 reduce-scatter.8.cloned.1.call-start
  507.9 1.3 copy-done.1
  509.2 0.8 fusion.13
  510.0 0.1 copy.75
  510.1 63.0 %reduce-scatter.4.cloned.1.call-done = bf16[256,256]{1,0:T(8,128)(2,1)} async-done(((bf16[4096,256]{1,0:T(8,128)(2,1)}), bf16[256,256]{1,0:T(8,128)(2,1)}) %reduce-scatter.4.cloned.1.call-update) | async-done | bytes 131088 | tf_op jit(solution)/shard_map/reduce_scatter | solution.py:116
  573.1 86.3 %reduce-scatter.6.cloned.1.call-done = bf16[256,256]{1,0:T(8,128)(2,1)} async-done(((bf16[4096,256]{1,0:T(8,128)(2,1)}), bf16[256,256]{1,0:T(8,128)(2,1)}) %reduce-scatter.6.cloned.1.call-update) | async-done | bytes 131088 | tf_op jit(solution)/shard_map/reduce_scatter | solution.py:119
  659.5 1.0 pad_maximum_fusion
  660.5 0.2 copy.76
  660.7 10.4 %convolution_convert_fusion = bf16[256,7168]{0,1:T(8,128)(2,1)} fusion(bf16[256,768]{0,1:T(8,128)(2,1)S(1)} %bitcast.110, bf16[7168,768]{0,1:T(8,128)(2,1)} %reshape_reshape.3), kind=kOutput, calls=%fused_computation.3 | convolution fusion | flops 2820407296 | bytes 15073280 | tf_op jit(solution)/shard_map/dot_general | solution.py:127
  671.1 100.1 %reduce-scatter.8.cloned.1.call-done = bf16[256,448]{0,1:T(8,128)(2,1)} async-done(((bf16[256,7168]{0,1:T(8,128)(2,1)}), bf16[256,448]{0,1:T(8,128)(2,1)}) %reduce-scatter.8.cloned.1.call-update) | async-done | bytes 229392 | tf_op jit(solution)/shard_map/reduce_scatter | solution.py:130
  (33 shorter events, 0.3 us)
Async XLA Ops:
  6.5 374.8 %all-gather.5.cloned.1.call-start = ((), (), s32[]{:S(2)}) async-start(), calls=%async_computation.7 | async-start | bytes 2228224 | tf_op jit(solution)/shard_map/all_gather | solution.py:109
  298.0 10.3 %copy-start.8 = (s32[8,4]{0,1:T(4,128)S(1)}, s32[8,4]{0,1:T(4,128)}, u32[]{:S(2)}) copy-start(s32[8,4]{0,1:T(4,128)} %param.6) | copy-start | bytes 388
  298.0 10.5 %copy-start.4 = (bf16[256,256]{1,0:T(8,128)(2,1)S(1)}, bf16[256,256]{1,0:T(8,128)(2,1)}, u32[]{:S(2)}) copy-start(bf16[256,256]{1,0:T(8,128)(2,1)} %param.7) | copy-start | bytes 393220
  307.2 149.4 %all-gather.7.cloned.1.call-start = ((), (), s32[]{:S(2)}) async-start(), calls=%async_computation.8 | async-start | bytes 2228224 | tf_op jit(solution)/shard_map/all_gather | solution.py:110
  308.0 265.1 %reduce-scatter.4.cloned.1.call-start = ((), (), s32[]{:S(2)}) async-start(), calls=%async_computation.4 | async-start | bytes 2228224 | tf_op jit(solution)/shard_map/reduce_scatter | solution.py:116
  461.4 3.5 copy-start.5
  461.5 3.5 copy-start.6
  468.5 3.0 copy-start.2
  468.5 3.8 copy-start.3
  472.3 2.1 copy-start.7
  473.0 1.4 copy-start
  489.8 169.7 %reduce-scatter.6.cloned.1.call-start = ((), (), s32[]{:S(2)}) async-start(), calls=%async_computation.5 | async-start | bytes 2228224 | tf_op jit(solution)/shard_map/reduce_scatter | solution.py:119
  507.6 1.6 copy-start.1
  507.6 263.5 %reduce-scatter.8.cloned.1.call-start = ((), (), s32[]{:S(2)}) async-start(), calls=%async_computation.6 | async-start | bytes 3899392 | tf_op jit(solution)/shard_map/reduce_scatter | solution.py:130
Sparse Core Ops, SparseCore 0:
  307.4 73.9 all-gather.4
  383.1 73.4 all-gather.6
  489.9 83.1 reduce-scatter.3
  575.5 83.9 reduce-scatter.5
  671.2 99.9 reduce-scatter.7
